TPU v7x, 32 devices: a whole 2x2x4 slice. The times are simulated.
32 devices in a mesh: sub: 8 (over y, x, core), row: 4 (over z).
Axes of the slice: x: 2, y: 2, z: 4, core: 2. Of those that a mesh axis runs over, the one named last changes fastest.
Arguments:
- band: float32 [16384, 1024], P(('sub', 'row')), parts along dimension 0, as said below
- precond: float32 [16384, 128], P(('sub', 'row')), parts along dimension 0, as said below
- half_band: int32 [8], P('sub'), parts along dimension 0, may hold values from 64 to 256
- interface: float32 [16384, 512], P(('sub', 'row')), parts along dimension 0, may hold values from -6 to 6
Outputs:
- modes: float32 [16384, 512], P(('sub', 'row')), parts along dimension 0
There are 8 independent parts, one for each index of `sub`. A program takes and returns all parts, laid end to end along the dimension named above; each array names one. Nothing has to cross between parts.
Inputs may be any that keep to these rules, and one draw needn't show every extreme that they name: band is symmetric as a stiffness: the entry coupling rows r and s equals that coupling s and r; entries at offset 0 lie in 0.05 to 0.5; entries beyond offset 256 or outside the matrix are 0; all entries are nonnegative. `precond`: every block is a symmetric positive definite 128 x 128 matrix.
All inputs are finite; a program needn't handle non-finite values.
Results may differ from a plain program's by a relative error of at most 0.0001.
Values sent between devices are 32-bit elements; how exact they have to be, the bound alone decides.
A program may use at most 64 MiB of HBM per device.

v0:
```python
import jax
import jax.numpy as jnp
from jax import lax
from jax.sharding import PartitionSpec as P

BAND = 256
BLOCK = 128
ITERS = 3


def with_halo(block, sides, width):
    for axis, dim in sides:
        count = lax.axis_size(axis)
        forward = [(i, i + 1) for i in range(count - 1)]
        backward = [(target, source) for source, target in forward]
        low = lax.ppermute(
            lax.slice_in_dim(block, block.shape[dim] - width, None, axis=dim), axis, forward
        )
        high = lax.ppermute(lax.slice_in_dim(block, 0, width, axis=dim), axis, backward)
        block = jnp.concatenate([low, block, high], axis=dim)
    return block


def couplings(band, half_band):
    width = band.shape[1]
    local_rows = jnp.arange(band.shape[0], dtype=jnp.int32)
    offsets = jnp.arange(width, dtype=jnp.int32)[None, :] - BAND - local_rows[:, None]
    reach = jnp.abs(offsets)
    inside = (reach >= 1) & (reach <= half_band[0])
    coupling = jnp.where(inside, band, jnp.zeros_like(band))
    diagonal = jnp.sum(coupling, axis=1) + jnp.sum(
        jnp.where(offsets == 0, band, jnp.zeros_like(band)), axis=1
    )
    return (coupling, diagonal)


def matmul(left, right):
    return jnp.dot(left, right, precision=lax.Precision.HIGHEST, preferred_element_type=jnp.float32)


def stiffness(vector, coupling, diagonal):
    padded = with_halo(vector, (("row", 0),), BAND)
    return diagonal[:, None] * vector - matmul(coupling, padded)


def precondition(vector, precond):
    blocks = vector.shape[0] // BLOCK
    matrices = precond.reshape(blocks, BLOCK, BLOCK)
    pieces = vector.reshape(blocks, BLOCK, vector.shape[1])
    return jnp.einsum("bij,bjm->bim", matrices, pieces, precision=lax.Precision.HIGHEST).reshape(
        vector.shape
    )


def paired_energy(residual, precond_res, image):
    return lax.psum(
        (jnp.sum(residual * precond_res, axis=0), jnp.sum(precond_res * image, axis=0)), "row"
    )


def per_device(band, precond, half_band, interface):
    coupling, diagonal = couplings(band, half_band)
    residual = -interface
    modes = jnp.zeros_like(interface)
    precond_res = precondition(residual, precond)
    image = stiffness(precond_res, coupling, diagonal)
    energy, product = paired_energy(residual, precond_res, image)
    step_len = energy / product
    direction = precond_res
    along = image
    for iteration in range(ITERS):
        modes = modes + step_len[None, :] * direction
        residual = residual - step_len[None, :] * along
        if iteration + 1 < ITERS:
            precond_res = precondition(residual, precond)
            image = stiffness(precond_res, coupling, diagonal)
            energy_next, product = paired_energy(residual, precond_res, image)
            ratio = energy_next / energy
            step_len = energy_next / (product - ratio * energy_next / step_len)
            direction = precond_res + ratio[None, :] * direction
            along = image + ratio[None, :] * along
            energy = energy_next
    return modes


def solution(mesh):
    return jax.shard_map(
        per_device,
        mesh=mesh,
        in_specs=(
            P(("sub", "row"), None),
            P(("sub", "row"), None),
            P("sub"),
            P(("sub", "row"), None),
        ),
        out_specs=P(("sub", "row"), None),
        check_vma=False,
    )
```

profile of v0, /device:TPU:0, one launch (start us, length us, event | category | flops | bytes accessed | tf_op | source)
XLA Modules:
  0.0 102.4 jit_solution(13549992620182338773)
XLA Ops:
  0.0 0.0 copy-start
  0.0 1.4 %neg.3 = f32[512,512]{1,0:T(8,128)S(1)} negate(f32[512,512]{1,0:T(8,128)} %param.7) | non-fusion elementwise | flops 262144 | bytes 2097152 | tf_op jit(solution)/shard_map/neg | solution.py:63
  1.4 0.0 copy-done
  1.4 0.0 copy-start.3
  1.4 1.0 fusion.50
  2.4 0.0 copy-start.2
  2.4 0.1 fusion.49
  2.5 1.4 %collective-permute-start.1 = (f32[256,512]{1,0:T(8,128)S(1)}, f32[256,512]{1,0:T(8,128)S(1)}, u32[]{:S(2)}, u32[]{:S(2)}) collective-permute-start(f32[256,512]{1,0:T(8,128)S(1)} %bitcast.48), channel_id=1, source_target_pairs={{1,0},{2,1},{3,2},{5,4},{6,5},{7,6},{9,8},{10,9},{11,10},{13,12},{... | collective-permute-start | bytes 1572872 | tf_op jit(solution)/shard_map/ppermute | solution.py:19
  3.9 5.6 %collective-permute-start = (f32[256,512]{1,0:T(8,128)S(1)}, f32[256,512]{1,0:T(8,128)S(1)}, u32[]{:S(2)}, u32[]{:S(2)}) collective-permute-start(f32[256,512]{1,0:T(8,128)S(1)} %bitcast.47), channel_id=1, source_target_pairs={{0,1},{1,2},{2,3},{4,5},{5,6},{6,7},{8,9},{9,10},{10,11},{12,13},{... | collective-permute-start | bytes 1572872 | tf_op jit(solution)/shard_map/ppermute | solution.py:16
  10.2 0.0 copy-done.3
  10.2 1.0 select_reduce_fusion
  11.2 8.3 %collective-permute-done.1 = f32[256,512]{1,0:T(8,128)S(1)} collective-permute-done((f32[256,512]{1,0:T(8,128)S(1)}, f32[256,512]{1,0:T(8,128)S(1)}, u32[]{:S(2)}, u32[]{:S(2)}) %collective-permute-start.1) | collective-permute-done | bytes 524320 | tf_op jit(solution)/shard_map/ppermute | solution.py:19
  19.5 1.2 %collective-permute-done = f32[256,512]{1,0:T(8,128)S(1)} collective-permute-done((f32[256,512]{1,0:T(8,128)S(1)}, f32[256,512]{1,0:T(8,128)S(1)}, u32[]{:S(2)}, u32[]{:S(2)}) %collective-permute-start) | collective-permute-done | bytes 524320 | tf_op jit(solution)/shard_map/ppermute | solution.py:16
  20.7 0.0 copy-done.2
  20.7 4.2 %multiply_reduce_fusion.3 = (f32[512]{0:T(512)S(1)}, f32[512]{0:T(512)S(1)}, f32[512,512]{1,0:T(8,128)S(1)}) fusion(f32[4,128,512]{2,1,0:T(8,128)S(1)} %fusion.50, f32[512,512]{1,0:T(8,128)S(1)} %copy-done.2, f32[256,512]{1,0:T(8,128)S(1)} %collective-permute-done.1, f32[512,512]{1,0:T(8,128)S(1)} %bitcast.43, f32[256,512]{1,0:T(8,128)S(1)} %collective-permute-done, ...), kind=kOutput, calls=%fused_computation.37 | convolution fusion | flops 3227253760 | bytes 7350276 | tf_op jit(solution)/shard_map/dot_general | solution.py:38
  24.9 0.0 copy-start.1
  24.9 13.1 %all-reduce.2 = (f32[512]{0:T(512)S(1)}, f32[512]{0:T(512)S(1)}) all-reduce(f32[512]{0:T(512)S(1)} %get-tuple-element.10, f32[512]{0:T(512)S(1)} %get-tuple-element.9), channel_id=1, replica_groups=mesh['sub'=8,'row'=4] {'row'}, use_global_device_ids=true, to_apply=%region_1.2 | all-reduce | flops 1024 | bytes 8192 | tf_op jit(solution)/shard_map/psum | solution.py:56
  38.0 1.5 %multiply_subtract_fusion.1 = f32[512,512]{1,0:T(8,128)S(1)} fusion(f32[512,512]{1,0:T(8,128)S(1)} %get-tuple-element.27, f32[512]{0:T(512)S(1)} %div.21, f32[512,512]{1,0:T(8,128)} %param.7), kind=kLoop, calls=%fused_computation.36 | loop fusion | flops 786432 | bytes 3147776 | tf_op jit(solution)/shard_map/sub | solution.py:73
  39.4 0.0 copy-done.1
  39.4 0.0 copy-start.4
  39.4 1.0 %fusion.51 = f32[4,512,128]{1,2,0:T(8,128)S(1)} fusion(f32[4,128,512]{2,1,0:T(8,128)S(1)} %bitcast.42, f32[4,128,128]{2,1,0:T(8,128)S(1)} %bitcast.37), kind=kOutput, calls=%fused_computation.51 | convolution fusion | flops 402653184 | bytes 2359296 | tf_op jit(solution)/shard_map/bij,bjm->bim/dot_general | solution.py:50
  40.5 0.1 fusion.48
  40.6 1.3 %collective-permute-start.3 = (f32[256,512]{1,0:T(8,128)S(1)}, f32[256,512]{1,0:T(8,128)S(1)}, u32[]{:S(2)}, u32[]{:S(2)}) collective-permute-start(f32[256,512]{1,0:T(8,128)S(1)} %bitcast.52), channel_id=1, source_target_pairs={{1,0},{2,1},{3,2},{5,4},{6,5},{7,6},{9,8},{10,9},{11,10},{13,12},{... | collective-permute-start | bytes 1572872 | tf_op jit(solution)/shard_map/ppermute | solution.py:19
  41.9 4.6 %collective-permute-start.2 = (f32[256,512]{1,0:T(8,128)S(1)}, f32[256,512]{1,0:T(8,128)S(1)}, u32[]{:S(2)}, u32[]{:S(2)}) collective-permute-start(f32[256,512]{1,0:T(8,128)S(1)} %bitcast.50), channel_id=1, source_target_pairs={{0,1},{1,2},{2,3},{4,5},{5,6},{6,7},{8,9},{9,10},{10,11},{12,13},{... | collective-permute-start | bytes 1572872 | tf_op jit(solution)/shard_map/ppermute | solution.py:16
  46.5 6.5 %collective-permute-done.3 = f32[256,512]{1,0:T(8,128)S(1)} collective-permute-done((f32[256,512]{1,0:T(8,128)S(1)}, f32[256,512]{1,0:T(8,128)S(1)}, u32[]{:S(2)}, u32[]{:S(2)}) %collective-permute-start.3) | collective-permute-done | bytes 524320 | tf_op jit(solution)/shard_map/ppermute | solution.py:19
  53.0 1.2 %collective-permute-done.2 = f32[256,512]{1,0:T(8,128)S(1)} collective-permute-done((f32[256,512]{1,0:T(8,128)S(1)}, f32[256,512]{1,0:T(8,128)S(1)}, u32[]{:S(2)}, u32[]{:S(2)}) %collective-permute-start.2) | collective-permute-done | bytes 524320 | tf_op jit(solution)/shard_map/ppermute | solution.py:16
  54.2 0.0 copy-done.4
  54.2 5.1 %multiply_reduce_fusion.1 = (f32[512]{0:T(512)S(1)}, f32[512]{0:T(512)S(1)}, f32[512,512]{1,0:T(8,128)}) fusion(f32[4,512,128]{1,2,0:T(8,128)S(1)} %fusion.51, f32[512,512]{1,0:T(8,128)S(1)} %multiply_subtract_fusion.1, f32[256,512]{1,0:T(8,128)S(1)} %collective-permute-done.3, f32[512,512]{1,0:T(8,128)S(1)} %bitcast.45, ...), kind=kOutput, calls=%fused_computation.34 | convolution fusion | flops 3226991616 | bytes 7350276 | tf_op jit(solution)/shard_map/dot_general | solution.py:38
  59.3 11.0 %all-reduce.1 = (f32[512]{0:T(512)S(1)}, f32[512]{0:T(512)S(1)}) all-reduce(f32[512]{0:T(512)S(1)} %get-tuple-element.8, f32[512]{0:T(512)S(1)} %get-tuple-element.7), channel_id=1, replica_groups=mesh['sub'=8,'row'=4] {'row'}, use_global_device_ids=true, to_apply=%region_7.8 | all-reduce | flops 1024 | bytes 8192 | tf_op jit(solution)/shard_map/psum | solution.py:56
  70.3 1.9 %multiply_subtract_fusion = f32[512,512]{1,0:T(8,128)S(1)} fusion(f32[512,512]{1,0:T(8,128)S(1)} %multiply_subtract_fusion.1, f32[512,512]{1,0:T(8,128)} %get-tuple-element.28, f32[512,512]{1,0:T(8,128)} %copy-done.1, f32[512]{0:T(512)S(1)} %get-tuple-element.20, f32[512]{0:T(512)S(1)} %get-tuple-element.19), kind=kLoop, calls=%fused_computation.33 | loop fusion | flops 1048576 | bytes 4198400 | tf_op jit(solution)/shard_map/sub | solution.py:73
  72.2 1.1 %fusion.52 = f32[4,512,128]{1,2,0:T(8,128)S(1)} fusion(f32[4,128,512]{2,1,0:T(8,128)S(1)} %bitcast.41, f32[4,128,128]{2,1,0:T(8,128)S(1)} %bitcast.38), kind=kOutput, calls=%fused_computation.52 | convolution fusion | flops 402653184 | bytes 2359296 | tf_op jit(solution)/shard_map/bij,bjm->bim/dot_general | solution.py:50
  73.3 0.0 copy-start.5
  73.3 0.1 fusion.47
  73.3 1.4 %collective-permute-start.5 = (f32[256,512]{1,0:T(8,128)S(1)}, f32[256,512]{1,0:T(8,128)S(1)}, u32[]{:S(2)}, u32[]{:S(2)}) collective-permute-start(f32[256,512]{1,0:T(8,128)S(1)} %bitcast.51), channel_id=1, source_target_pairs={{1,0},{2,1},{3,2},{5,4},{6,5},{7,6},{9,8},{10,9},{11,10},{13,12},{... | collective-permute-start | bytes 1572872 | tf_op jit(solution)/shard_map/ppermute | solution.py:19
  74.8 4.6 %collective-permute-start.4 = (f32[256,512]{1,0:T(8,128)S(1)}, f32[256,512]{1,0:T(8,128)S(1)}, u32[]{:S(2)}, u32[]{:S(2)}) collective-permute-start(f32[256,512]{1,0:T(8,128)S(1)} %bitcast.49), channel_id=1, source_target_pairs={{0,1},{1,2},{2,3},{4,5},{5,6},{6,7},{8,9},{9,10},{10,11},{12,13},{... | collective-permute-start | bytes 1572872 | tf_op jit(solution)/shard_map/ppermute | solution.py:16
  79.4 0.2 multiply_reduce_fusion
  79.5 5.0 %collective-permute-done.5 = f32[256,512]{1,0:T(8,128)S(1)} collective-permute-done((f32[256,512]{1,0:T(8,128)S(1)}, f32[256,512]{1,0:T(8,128)S(1)}, u32[]{:S(2)}, u32[]{:S(2)}) %collective-permute-start.5) | collective-permute-done | bytes 524320 | tf_op jit(solution)/shard_map/ppermute | solution.py:19
  84.6 1.5 %collective-permute-done.4 = f32[256,512]{1,0:T(8,128)S(1)} collective-permute-done((f32[256,512]{1,0:T(8,128)S(1)}, f32[256,512]{1,0:T(8,128)S(1)}, u32[]{:S(2)}, u32[]{:S(2)}) %collective-permute-start.4) | collective-permute-done | bytes 524320 | tf_op jit(solution)/shard_map/ppermute | solution.py:16
  86.0 0.0 copy-done.5
  86.0 4.1 %fusion.36 = f32[512]{0:T(512)S(1)} fusion(f32[512,512]{1,0:T(8,128)S(1)} %bitcast.40, f32[256,512]{1,0:T(8,128)S(1)} %collective-permute-done.5, f32[256,512]{1,0:T(8,128)S(1)} %collective-permute-done.4, f32[512]{0:T(512)S(1)} %add.40, f32[512,1024]{1,0:T(8,128)S(1)} %copy-done.5, s32[]{:T(128)} %bitcast.33, s32[1024]{0:T(1024)S(1)} %iota_add_fusion), kind=kOutput, calls=%fused_computation.30 | convolution fusion | flops 3226467840 | bytes 4202500 | tf_op jit(solution)/shard_map/dot_general | solution.py:38
  90.1 10.9 %all-reduce = (f32[512]{0:T(512)S(1)}, f32[512]{0:T(512)S(1)}) all-reduce(f32[512]{0:T(512)S(1)} %multiply_reduce_fusion, f32[512]{0:T(512)S(1)} %fusion.36), channel_id=1, replica_groups=mesh['sub'=8,'row'=4] {'row'}, use_global_device_ids=true, to_apply=%region_11.12 | all-reduce | flops 1024 | bytes 8192 | tf_op jit(solution)/shard_map/psum | solution.py:56
  101.0 1.4 %multiply_add_fusion = f32[512,512]{1,0:T(8,128)} fusion(f32[512]{0:T(512)S(1)} %get-tuple-element.18, f32[512]{0:T(512)S(1)} %get-tuple-element.17, f32[512]{0:T(512)S(1)} %get-tuple-element.20, f32[512]{0:T(512)S(1)} %get-tuple-element.19, f32[512]{0:T(512)S(1)} %div.21, f32[4,512,128]{1,2,0:T(8,128)S(1)} %fusion.52, f32[4,512,128]{1,2,0:T(8,128)S(1)} %fusion.51, ...), kind=kLoop, calls=%fused_computation.31 | loop fusion | flops 2359296 | bytes 4204544 | tf_op jit(solution)/shard_map/add | solution.py:72
  (5 shorter events, 0.0 us)
Async XLA Ops:
  0.0 1.4 %copy-start = (f32[512,128]{1,0:T(8,128)S(1)}, f32[512,128]{1,0:T(8,128)}, u32[]{:S(2)}) copy-start(f32[512,128]{1,0:T(8,128)} %param.5) | copy-start | bytes 786436
  1.4 8.8 %copy-start.3 = (f32[512,1024]{1,0:T(8,128)S(1)}, f32[512,1024]{1,0:T(8,128)}, u32[]{:S(2)}) copy-start(f32[512,1024]{1,0:T(8,128)} %param.4) | copy-start | bytes 6291460
  2.4 18.3 %copy-start.2 = (f32[512,512]{1,0:T(8,128)S(1)}, f32[512,512]{1,0:T(8,128)}, u32[]{:S(2)}) copy-start(f32[512,512]{1,0:T(8,128)} %param.7) | copy-start | bytes 3145732
  2.5 17.0 %collective-permute-start.1 = (f32[256,512]{1,0:T(8,128)S(1)}, f32[256,512]{1,0:T(8,128)S(1)}, u32[]{:S(2)}, u32[]{:S(2)}) collective-permute-start(f32[256,512]{1,0:T(8,128)S(1)} %bitcast.48), channel_id=1, source_target_pairs={{1,0},{2,1},{3,2},{5,4},{6,5},{7,6},{9,8},{10,9},{11,10},{13,12},{... | collective-permute-start | bytes 1572872 | tf_op jit(solution)/shard_map/ppermute | solution.py:19
  3.9 16.8 %collective-permute-start = (f32[256,512]{1,0:T(8,128)S(1)}, f32[256,512]{1,0:T(8,128)S(1)}, u32[]{:S(2)}, u32[]{:S(2)}) collective-permute-start(f32[256,512]{1,0:T(8,128)S(1)} %bitcast.47), channel_id=1, source_target_pairs={{0,1},{1,2},{2,3},{4,5},{5,6},{6,7},{8,9},{9,10},{10,11},{12,13},{... | collective-permute-start | bytes 1572872 | tf_op jit(solution)/shard_map/ppermute | solution.py:16
  24.9 14.5 %copy-start.1 = (f32[512,512]{1,0:T(8,128)}, f32[512,512]{1,0:T(8,128)S(1)}, u32[]{:S(2)}) copy-start(f32[512,512]{1,0:T(8,128)S(1)} %get-tuple-element.27) | copy-start | bytes 3145732
  39.4 14.7 %copy-start.4 = (f32[512,1024]{1,0:T(8,128)S(1)}, f32[512,1024]{1,0:T(8,128)}, u32[]{:S(2)}) copy-start(f32[512,1024]{1,0:T(8,128)} %param.4) | copy-start | bytes 6291460
  40.6 12.4 %collective-permute-start.3 = (f32[256,512]{1,0:T(8,128)S(1)}, f32[256,512]{1,0:T(8,128)S(1)}, u32[]{:S(2)}, u32[]{:S(2)}) collective-permute-start(f32[256,512]{1,0:T(8,128)S(1)} %bitcast.52), channel_id=1, source_target_pairs={{1,0},{2,1},{3,2},{5,4},{6,5},{7,6},{9,8},{10,9},{11,10},{13,12},{... | collective-permute-start | bytes 1572872 | tf_op jit(solution)/shard_map/ppermute | solution.py:19
  41.9 12.3 %collective-permute-start.2 = (f32[256,512]{1,0:T(8,128)S(1)}, f32[256,512]{1,0:T(8,128)S(1)}, u32[]{:S(2)}, u32[]{:S(2)}) collective-permute-start(f32[256,512]{1,0:T(8,128)S(1)} %bitcast.50), channel_id=1, source_target_pairs={{0,1},{1,2},{2,3},{4,5},{5,6},{6,7},{8,9},{9,10},{10,11},{12,13},{... | collective-permute-start | bytes 1572872 | tf_op jit(solution)/shard_map/ppermute | solution.py:16
  73.3 12.8 %copy-start.5 = (f32[512,1024]{1,0:T(8,128)S(1)}, f32[512,1024]{1,0:T(8,128)}, u32[]{:S(2)}) copy-start(f32[512,1024]{1,0:T(8,128)} %param.4) | copy-start | bytes 6291460
  73.3 11.2 %collective-permute-start.5 = (f32[256,512]{1,0:T(8,128)S(1)}, f32[256,512]{1,0:T(8,128)S(1)}, u32[]{:S(2)}, u32[]{:S(2)}) collective-permute-start(f32[256,512]{1,0:T(8,128)S(1)} %bitcast.51), channel_id=1, source_target_pairs={{1,0},{2,1},{3,2},{5,4},{6,5},{7,6},{9,8},{10,9},{11,10},{13,12},{... | collective-permute-start | bytes 1572872 | tf_op jit(solution)/shard_map/ppermute | solution.py:19
  74.8 11.2 %collective-permute-start.4 = (f32[256,512]{1,0:T(8,128)S(1)}, f32[256,512]{1,0:T(8,128)S(1)}, u32[]{:S(2)}, u32[]{:S(2)}) collective-permute-start(f32[256,512]{1,0:T(8,128)S(1)} %bitcast.49), channel_id=1, source_target_pairs={{0,1},{1,2},{2,3},{4,5},{5,6},{6,7},{8,9},{9,10},{10,11},{12,13},{... | collective-permute-start | bytes 1572872 | tf_op jit(solution)/shard_map/ppermute | solution.py:16
where the time goes:
time: 103 us; the launch traced here: 102 us
  blocking collectives  34.9 us (34%)
  waiting for transfers between devices  23.6 us (23%)
  starting transfers between devices  18.9 us (18%)
  matrix products  16.5 us (16%)
  other arithmetic  7.35 us (7%)
    psum x3, blocking collectives, paired_energy(): lax.psum((jnp.sum(residual * precond_res, axis=0), jnp.sum(precond_res *...  34.9 us
    ppermute x3, waiting for transfers between devices, with_halo(): lax.ppermute(lax.slice_in_dim(block, 0, width, axis=dim), axis, backward)  19.8 us
    ppermute x3, starting transfers between devices, with_halo(): lax.ppermute(lax.slice_in_dim(block, block.shape[dim] - width, None, axis...  14.8 us
    dot_general x3, matrix products, matmul(): jnp.dot(left, right, precision=lax.Precision.HIGHEST, preferred_element_t...  13.4 us
    ppermute x3, starting transfers between devices, with_halo(): lax.ppermute(lax.slice_in_dim(block, 0, width, axis=dim), axis, backward)  4.14 us
    ppermute x3, waiting for transfers between devices, with_halo(): lax.ppermute(lax.slice_in_dim(block, block.shape[dim] - width, None, axis...  3.82 us
    sub x2, other arithmetic, per_device(): residual = residual - step_len[None, :] * along  3.38 us
    dot_general x3, matrix products, precondition(): jnp.einsum('bij,bjm->bim', matrices, pieces, precision=lax.Precision.HIGH...  3.09 us
  transfers between devices with their start and end apart: 6, of which 6 were waited for; matrix products, arithmetic and copies ran while one was open for 1% of the time, Pallas kernels for 0%

commit v1 on v0

v1 whole, which is shorter than its diff:
```python
import functools

import jax
import jax.numpy as jnp
from jax import lax
from jax.experimental import pallas as pl
from jax.experimental.pallas import tpu as pltpu
from jax.sharding import PartitionSpec as P

MESH = pl.DeviceIdType.MESH
CHUNK = 256
F32 = jnp.float32
BF16 = jnp.bfloat16


def split(value):
    high = value.astype(BF16)
    return high, (value - high.astype(F32)).astype(BF16)


def dot(left, right):
    return jnp.dot(left, right, preferred_element_type=F32)


def dot3(left_hi, left_lo, right_hi, right_lo):
    return dot(left_hi, right_hi) + dot(left_lo, right_hi) + dot(left_hi, right_lo)


def kernel(
    n,
    band_hbm,
    precond_hbm,
    half_ref,
    rhs_hbm,
    out_hbm,
    band,
    precond,
    rhs,
    out,
    chi,
    clo,
    pcat,
    diag,
    z0,
    w0,
    z1,
    w1,
    u,
    vhi,
    vlo,
    halo0,
    halo1,
    halo2,
    red0,
    red1,
    in_sem,
    out_sem,
    send_sem,
    recv_sem,
    rsend_sem,
    rrecv_sem,
):
    me = lax.axis_index("row")
    rows, width = band.shape
    edge = (width - rows) // 2
    block = precond.shape[1]
    chunks = rhs.shape[0]
    half = CHUNK // 2
    low_rows, high_rows = slice(0, edge), slice(rows - edge, rows)
    low_cols, mid_cols, high_cols = slice(0, edge), slice(edge, edge + rows), slice(edge + rows, width)

    loads = [pltpu.make_async_copy(precond_hbm, precond, in_sem.at[0])]
    for c in range(chunks):
        loads.append(
            pltpu.make_async_copy(
                rhs_hbm.at[:, pl.ds(c * CHUNK, CHUNK)], rhs.at[c], in_sem.at[2 + c]
            )
        )
    loads.append(pltpu.make_async_copy(band_hbm, band, in_sem.at[1]))
    for load in loads:
        load.start()

    barrier = pltpu.get_barrier_semaphore()
    for k in range(1, n):
        pl.semaphore_signal(
            barrier, inc=1, device_id={"row": lax.rem(me + k, n)}, device_id_type=MESH
        )

    def exchange(stage, c):
        if stage < 2:
            source, halo = (z0, halo0) if stage == 0 else (z1, halo1)
            down = (source.at[c, low_rows], halo.at[c, 1])
            up = (source.at[c, high_rows], halo.at[c, 0])
        else:
            down = (u.at[c, low_rows, pl.ds(0, half)], halo2.at[c, 1])
            up = (u.at[c, high_rows, pl.ds(half, half)], halo2.at[c, 0])
        to_low = pltpu.make_async_remote_copy(
            src_ref=down[0],
            dst_ref=down[1],
            send_sem=send_sem.at[stage, c, 0],
            recv_sem=recv_sem.at[stage, c, 1],
            device_id={"row": lax.rem(me + n - 1, n)},
            device_id_type=MESH,
        )
        to_high = pltpu.make_async_remote_copy(
            src_ref=up[0],
            dst_ref=up[1],
            send_sem=send_sem.at[stage, c, 1],
            recv_sem=recv_sem.at[stage, c, 0],
            device_id={"row": lax.rem(me + 1, n)},
            device_id_type=MESH,
        )
        return to_low, to_high

    def send(stage, c):
        to_low, to_high = exchange(stage, c)
        pl.when(me > 0)(to_low.start)
        pl.when(me < n - 1)(to_high.start)

    def receive(stage, c):
        to_low, to_high = exchange(stage, c)
        pl.when(me < n - 1)(to_low.wait_recv)
        pl.when(me > 0)(to_high.wait_recv)

    def sums(which, c):
        buffer = red0 if which == 0 else red1
        copies = []
        for k in range(1, n):
            copies.append(
                pltpu.make_async_remote_copy(
                    src_ref=buffer.at[c, me],
                    dst_ref=buffer.at[c, me],
                    send_sem=rsend_sem.at[which, c, k - 1],
                    recv_sem=rrecv_sem.at[which, c, k - 1],
                    device_id={"row": lax.rem(me + k, n)},
                    device_id_type=MESH,
                )
            )
        return copies

    def send_sums(which, c, values):
        buffer = red0 if which == 0 else red1
        for index, value in enumerate(values):
            buffer[c, me, index : index + 1, :] = value
        for copy in sums(which, c):
            copy.start()

    def receive_sums(which, c):
        for copy in sums(which, c):
            copy.wait_recv()
        buffer = red0 if which == 0 else red1
        total = buffer[c, 0]
        for source in range(1, n):
            total = total + buffer[c, source]
        return total

    def colsum(value):
        return jnp.sum(value, axis=0, keepdims=True)

    def apply_precond(c, source, target):
        for b in range(rows // block):
            at = slice(b * block, (b + 1) * block)
            high, low = split(source[c, at])
            product = dot(pcat[at], jnp.concatenate([high, high], axis=0)) + dot(
                pcat[at, 0:block], low
            )
            target[c, at] = product

    def local_image(c, source, target):
        high, low = split(source[c])
        vhi[c] = high
        vlo[c] = low
        for b in range(rows // edge):
            at = slice(b * edge, (b + 1) * edge)
            coupled = dot3(chi[at, mid_cols], clo[at, mid_cols], vhi[c], vlo[c])
            target[c, at] = diag[at] * source[c, at] - coupled

    def edge_image(c, halo, target):
        for side, at, cols in ((0, low_rows, low_cols), (1, high_rows, high_cols)):
            high, low = split(halo[c, side])
            target[c, at] = target[c, at] - dot3(chi[at, cols], clo[at, cols], high, low)

    @pl.when(me == 0)
    def _():
        for c in range(chunks):
            for halo in (halo0, halo1, halo2):
                halo[c, 0] = jnp.zeros(halo.shape[2:], F32)

    @pl.when(me == n - 1)
    def _():
        for c in range(chunks):
            for halo in (halo0, halo1, halo2):
                halo[c, 1] = jnp.zeros(halo.shape[2:], F32)

    loads[0].wait()
    high, low = split(precond[...])
    pcat[:, 0:block] = high
    pcat[:, block : 2 * block] = low
    for c in range(chunks):
        loads[1 + c].wait()
        apply_precond(c, rhs, z0)
        if c == 0:
            pl.semaphore_wait(barrier, n - 1)
        send(0, c)

    loads[-1].wait()
    reach_max = half_ref[0]
    for b in range(rows // block):
        at = slice(b * block, (b + 1) * block)
        values = band[at]
        offsets = (
            lax.broadcasted_iota(jnp.int32, values.shape, 1)
            - edge
            - b * block
            - lax.broadcasted_iota(jnp.int32, values.shape, 0)
        )
        reach = jnp.abs(offsets)
        kept = jnp.where(reach <= reach_max, values, 0.0)
        diag[at] = jnp.sum(kept, axis=1, keepdims=True)
        coupling = jnp.where(reach >= 1, kept, 0.0)
        high, low = split(coupling)
        chi[at] = high
        clo[at] = low

    for c in range(chunks):
        local_image(c, z0, w0)
    for c in range(chunks):
        receive(0, c)
        edge_image(c, halo0, w0)
        apply_precond(c, w0, z1)
        send(1, c)
        send_sums(0, c, [colsum(rhs[c] * z0[c]), colsum(z0[c] * w0[c])])
        local_image(c, z1, w1)

    first = []
    for c in range(chunks):
        receive(1, c)
        edge_image(c, halo1, w1)
        total = receive_sums(0, c)
        energy, product = total[0:1], total[1:2]
        step = energy / product
        first.append((energy, product, step))
        for b in range(rows // block):
            at = slice(b * block, (b + 1) * block)
            high, low = split(w1[c, at])
            z2 = dot(pcat[at], jnp.concatenate([high, high], axis=0)) + dot(pcat[at, 0:block], low)
            u[c, at] = z1[c, at] - step * z2
        send(2, c)

    partial = []
    for c in range(chunks):
        step = first[c][2]
        terms = None
        high, low = split(u[c])
        vhi[c] = high
        vlo[c] = low
        for b in range(rows // block):
            at = slice(b * block, (b + 1) * block)
            residual = rhs[c, at] - step * w0[c, at]
            pres = z0[c, at] - step * z1[c, at]
            image = w0[c, at] - step * w1[c, at]
            ub = u[c, at]
            coupled = dot3(chi[at, mid_cols], clo[at, mid_cols], vhi[c], vlo[c])
            new = [
                colsum(residual * pres),
                colsum(pres * image),
                colsum(ub * w0[c, at]),
                colsum(ub * residual),
                colsum(ub * image),
                colsum(ub * (diag[at] * ub - coupled)),
            ]
            terms = new if terms is None else [x + y for x, y in zip(terms, new)]
        partial.append(terms)

    for c in range(chunks):
        receive(2, c)
        sides = []
        for side, at, cols, lanes in (
            (1, high_rows, high_cols, slice(0, half)),
            (0, low_rows, low_cols, slice(half, CHUNK)),
        ):
            high, low = split(halo2[c, side])
            coupled = dot3(chi[at, cols], clo[at, cols], high, low)
            sides.append(colsum(u[c, at, lanes] * coupled))
        terms = partial[c]
        terms[5] = terms[5] - 2.0 * jnp.concatenate(sides, axis=1)
        send_sums(1, c, terms)

    stores = []
    for c in range(chunks):
        energy, product, step = first[c]
        total = receive_sums(1, c)
        energy1, image1, uw, ur, ui, uku = [total[i : i + 1] for i in range(6)]
        ratio = energy1 / energy
        product1 = image1 - ratio * energy1 / step
        step1 = energy1 / product1
        along = ui + ratio * uw
        f0 = uw / product
        f1 = along / product1
        gamma = (ur - step1 * along) / (uku - f0 * uw - f1 * along)
        rest = step1 - gamma * f1
        cz0 = -(step - gamma * f0 + rest * (1.0 + ratio))
        cz1 = step * rest
        for b in range(rows // block):
            at = slice(b * block, (b + 1) * block)
            out[c, at] = cz0 * z0[c, at] + cz1 * z1[c, at] - gamma * u[c, at]
        store = pltpu.make_async_copy(
            out.at[c], out_hbm.at[:, pl.ds(c * CHUNK, CHUNK)], out_sem.at[c]
        )
        store.start()
        stores.append(store)

    for stage in range(3):
        for c in range(chunks):
            to_low, to_high = exchange(stage, c)
            pl.when(me > 0)(to_low.wait_send)
            pl.when(me < n - 1)(to_high.wait_send)
    for which in range(2):
        for c in range(chunks):
            for copy in sums(which, c):
                copy.wait_send()
    for store in stores:
        store.wait()


def solution(mesh):
    n = mesh.shape["row"]

    def per_device(band, precond, half_band, interface):
        rows, width = band.shape
        block = precond.shape[1]
        edge = (width - rows) // 2
        cols = interface.shape[1]
        chunks = cols // CHUNK
        full = pltpu.VMEM((chunks, rows, CHUNK), F32)
        any_spec = pl.BlockSpec(memory_space=pl.ANY)
        return pl.pallas_call(
            functools.partial(kernel, n),
            out_shape=jax.ShapeDtypeStruct((rows, cols), F32),
            in_specs=[any_spec, any_spec, pl.BlockSpec(memory_space=pltpu.SMEM), any_spec],
            out_specs=any_spec,
            scratch_shapes=[
                pltpu.VMEM((rows, width), F32),
                pltpu.VMEM((rows, block), F32),
                full,
                full,
                pltpu.VMEM((rows, width), BF16),
                pltpu.VMEM((rows, width), BF16),
                pltpu.VMEM((rows, 2 * block), BF16),
                pltpu.VMEM((rows, 1), F32),
                full,
                full,
                full,
                full,
                full,
                pltpu.VMEM((chunks, rows, CHUNK), BF16),
                pltpu.VMEM((chunks, rows, CHUNK), BF16),
                pltpu.VMEM((chunks, 2, edge, CHUNK), F32),
                pltpu.VMEM((chunks, 2, edge, CHUNK), F32),
                pltpu.VMEM((chunks, 2, edge, CHUNK // 2), F32),
                pltpu.VMEM((chunks, n, 8, CHUNK), F32),
                pltpu.VMEM((chunks, n, 8, CHUNK), F32),
                pltpu.SemaphoreType.DMA((2 + chunks,)),
                pltpu.SemaphoreType.DMA((chunks,)),
                pltpu.SemaphoreType.DMA((3, chunks, 2)),
                pltpu.SemaphoreType.DMA((3, chunks, 2)),
                pltpu.SemaphoreType.DMA((2, chunks, n - 1)),
                pltpu.SemaphoreType.DMA((2, chunks, n - 1)),
            ],
            compiler_params=pltpu.CompilerParams(
                collective_id=0, has_side_effects=True, vmem_limit_bytes=48 * 1024 * 1024
            ),
        )(band, precond, half_band, interface)

    return jax.shard_map(
        per_device,
        mesh=mesh,
        in_specs=(
            P(("sub", "row"), None),
            P(("sub", "row"), None),
            P("sub"),
            P(("sub", "row"), None),
        ),
        out_specs=P(("sub", "row"), None),
        check_vma=False,
    )
```

time: 103 us -> 46.7 us (0.45)
  Pallas kernels: 0 us -> 41.1 us
  blocking collectives: 34.9 us -> 0 us
  waiting for transfers between devices: 23.6 us -> 0 us
  starting transfers between devices: 18.9 us -> 0 us
  matrix products: 16.5 us -> 0 us
  other arithmetic: 7.35 us -> 0 us
  local copies, waits for them, and re-layouts: 0.25 us -> 4.73 us
    pallas_call x0 -> x1, Pallas kernels: none -> 41.1 us  [per_device(): pl.pallas_call(functools.partial(kernel, n), out_shape=jax.ShapeDtypeStru...]
    psum x3 -> x0, blocking collectives: 34.9 us -> none  [paired_energy(): lax.psum((jnp.sum(residual * precond_res, axis=0), jnp.sum(precond_res *...]
    ppermute x6 -> x0, waiting for transfers between devices: 23.6 us -> none  [the longest x3 19.8 us: with_halo(): lax.ppermute(lax.slice_in_dim(block, 0, width, axis=dim), axis, backward)]
    ppermute x6 -> x0, starting transfers between devices: 18.9 us -> none  [the longest x3 14.8 us: with_halo(): lax.ppermute(lax.slice_in_dim(block, block.shape[dim] - width, None, axis...]
    dot_general x6 -> x0, matrix products: 16.5 us -> none  [the longest x3 13.4 us: matmul(): jnp.dot(left, right, precision=lax.Precision.HIGHEST, preferred_element_t...]
    unnamed x12 -> x7, local copies, waits for them, and re-layouts: 0.03 us -> 4.73 us
    sub x3 -> x0, other arithmetic: 3.38 us -> none  [the longest x2 3.38 us: per_device(): residual = residual - step_len[None, :] * along]
    add x2 -> x0, other arithmetic: 1.38 us -> none  [the longest x1 1.37 us: per_device(): modes = modes + step_len[None, :] * direction]
  transfers between devices with their start and end apart: 6 -> 0, of which waited for: 6 -> 0; matrix products, arithmetic and copies ran while one was open for 1% -> 0% of each run, Pallas kernels for 0% -> 0%
where the time goes in v1:
time: 46.7 us; the launch traced here: 46.5 us
  Pallas kernels  41.1 us (88%)
  local copies, waits for them, and re-layouts  4.73 us (10%)
  between operations  0.67 us (1%)
    pallas_call x1, Pallas kernels, per_device(): pl.pallas_call(functools.partial(kernel, n), out_shape=jax.ShapeDtypeStru...  41.1 us
    unnamed x7, local copies, waits for them, and re-layouts  4.73 us

profile of v1, /device:TPU:0, one launch (start us, length us, event | category | flops | bytes accessed | tf_op | source)
XLA Modules:
  0.0 46.5 jit_solution(202269579098606281)
XLA Ops:
  0.7 0.0 copy-start
  0.7 1.6 %copy-done = f32[512,1024]{1,0:T(8,128)S(1)} copy-done((f32[512,1024]{1,0:T(8,128)S(1)}, f32[512,1024]{1,0:T(8,128)}, u32[]{:S(2)}) %copy-start) | copy-done | bytes 2097176
  2.2 0.0 copy-start.1
  2.2 1.2 %copy-done.1 = f32[512,512]{1,0:T(8,128)S(1)} copy-done((f32[512,512]{1,0:T(8,128)S(1)}, f32[512,512]{1,0:T(8,128)}, u32[]{:S(2)}) %copy-start.1) | copy-done | bytes 1048600
  3.5 0.0 copy-start.2
  3.5 0.9 %copy-done.2 = f32[512,128]{1,0:T(8,128)S(1)} copy-done((f32[512,128]{1,0:T(8,128)S(1)}, f32[512,128]{1,0:T(8,128)}, u32[]{:S(2)}) %copy-start.2) | copy-done | bytes 262168
  4.4 41.1 %shard_map.46 = f32[512,512]{1,0:T(8,128)S(1)} custom-call(f32[512,1024]{1,0:T(8,128)S(1)} %copy-done, f32[512,128]{1,0:T(8,128)S(1)} %copy-done.2, s32[1]{0:T(128)S(6)} %copy.6.half_ref, f32[512,512]{1,0:T(8,128)S(1)} %copy-done.1), custom_call_target="tpu_custom_call" | custom-call | tf_op jit(solution)/shard_map/pallas_call | solution.py:337
  45.5 1.0 %copy.7 = f32[512,512]{1,0:T(8,128)} copy(f32[512,512]{1,0:T(8,128)S(1)} %shard_map.46) | data formatting | bytes 2097152
Async XLA Ops:
  0.7 1.6 %copy-start = (f32[512,1024]{1,0:T(8,128)S(1)}, f32[512,1024]{1,0:T(8,128)}, u32[]{:S(2)}) copy-start(f32[512,1024]{1,0:T(8,128)} %band_hbm.1) | copy-start | bytes 6291460
  2.2 1.2 %copy-start.1 = (f32[512,512]{1,0:T(8,128)S(1)}, f32[512,512]{1,0:T(8,128)}, u32[]{:S(2)}) copy-start(f32[512,512]{1,0:T(8,128)} %rhs_hbm.1) | copy-start | bytes 3145732
  3.5 0.9 %copy-start.2 = (f32[512,128]{1,0:T(8,128)S(1)}, f32[512,128]{1,0:T(8,128)}, u32[]{:S(2)}) copy-start(f32[512,128]{1,0:T(8,128)} %precond_hbm.1) | copy-start | bytes 786436

commit v2 on v1

--- a/solution.py
+++ b/solution.py
@@ -32,11 +32,10 @@
     precond_hbm,
     half_ref,
     rhs_hbm,
-    out_hbm,
+    out_ref,
     band,
     precond,
     rhs,
-    out,
     chi,
     clo,
     pcat,
@@ -54,7 +53,6 @@
     red0,
     red1,
     in_sem,
-    out_sem,
     send_sem,
     recv_sem,
     rsend_sem,
@@ -65,8 +63,9 @@
     edge = (width - rows) // 2
     block = precond.shape[1]
     chunks = rhs.shape[0]
-    half = CHUNK // 2
+    half = edge // 2
     low_rows, high_rows = slice(0, edge), slice(rows - edge, rows)
+    near_low, near_high = slice(0, half), slice(rows - half, rows)
     low_cols, mid_cols, high_cols = slice(0, edge), slice(edge, edge + rows), slice(edge + rows, width)
 
     loads = [pltpu.make_async_copy(precond_hbm, precond, in_sem.at[0])]
@@ -77,7 +76,7 @@
             )
         )
     loads.append(pltpu.make_async_copy(band_hbm, band, in_sem.at[1]))
-    for load in loads:
+    for load in loads[:-1]:
         load.start()
 
     barrier = pltpu.get_barrier_semaphore()
@@ -92,8 +91,8 @@
             down = (source.at[c, low_rows], halo.at[c, 1])
             up = (source.at[c, high_rows], halo.at[c, 0])
         else:
-            down = (u.at[c, low_rows, pl.ds(0, half)], halo2.at[c, 1])
-            up = (u.at[c, high_rows, pl.ds(half, half)], halo2.at[c, 0])
+            down = (u.at[c, near_low], halo2.at[c, 1])
+            up = (u.at[c, near_high], halo2.at[c, 0])
         to_low = pltpu.make_async_remote_copy(
             src_ref=down[0],
             dst_ref=down[1],
@@ -198,6 +197,8 @@
     pcat[:, block : 2 * block] = low
     for c in range(chunks):
         loads[1 + c].wait()
+        if c == 0:
+            loads[-1].start()
         apply_precond(c, rhs, z0)
         if c == 0:
             pl.semaphore_wait(barrier, n - 1)
@@ -274,19 +275,16 @@
 
     for c in range(chunks):
         receive(2, c)
-        sides = []
-        for side, at, cols, lanes in (
-            (1, high_rows, high_cols, slice(0, half)),
-            (0, low_rows, low_cols, slice(half, CHUNK)),
+        terms = partial[c]
+        for side, at, cols in (
+            (0, low_rows, slice(half, edge)),
+            (1, slice(rows - edge, rows - half), slice(edge + rows, edge + rows + half)),
         ):
             high, low = split(halo2[c, side])
             coupled = dot3(chi[at, cols], clo[at, cols], high, low)
-            sides.append(colsum(u[c, at, lanes] * coupled))
-        terms = partial[c]
-        terms[5] = terms[5] - 2.0 * jnp.concatenate(sides, axis=1)
+            terms[5] = terms[5] - 2.0 * colsum(u[c, at] * coupled)
         send_sums(1, c, terms)
 
-    stores = []
     for c in range(chunks):
         energy, product, step = first[c]
         total = receive_sums(1, c)
@@ -303,12 +301,9 @@
         cz1 = step * rest
         for b in range(rows // block):
             at = slice(b * block, (b + 1) * block)
-            out[c, at] = cz0 * z0[c, at] + cz1 * z1[c, at] - gamma * u[c, at]
-        store = pltpu.make_async_copy(
-            out.at[c], out_hbm.at[:, pl.ds(c * CHUNK, CHUNK)], out_sem.at[c]
-        )
-        store.start()
-        stores.append(store)
+            out_ref[at, c * CHUNK : (c + 1) * CHUNK] = (
+                cz0 * z0[c, at] + cz1 * z1[c, at] - gamma * u[c, at]
+            )
 
     for stage in range(3):
         for c in range(chunks):
@@ -319,8 +314,6 @@
         for c in range(chunks):
             for copy in sums(which, c):
                 copy.wait_send()
-    for store in stores:
-        store.wait()
 
 
 def solution(mesh):
@@ -332,17 +325,19 @@
         edge = (width - rows) // 2
         cols = interface.shape[1]
         chunks = cols // CHUNK
+        band, precond, interface = (
+            pltpu.with_memory_space_constraint(x, pltpu.HBM) for x in (band, precond, interface)
+        )
         full = pltpu.VMEM((chunks, rows, CHUNK), F32)
         any_spec = pl.BlockSpec(memory_space=pl.ANY)
         return pl.pallas_call(
             functools.partial(kernel, n),
-            out_shape=jax.ShapeDtypeStruct((rows, cols), F32),
+            out_shape=pltpu.VMEM((rows, cols), F32),
             in_specs=[any_spec, any_spec, pl.BlockSpec(memory_space=pltpu.SMEM), any_spec],
-            out_specs=any_spec,
+            out_specs=pl.BlockSpec(memory_space=pltpu.VMEM),
             scratch_shapes=[
                 pltpu.VMEM((rows, width), F32),
                 pltpu.VMEM((rows, block), F32),
-                full,
                 full,
                 pltpu.VMEM((rows, width), BF16),
                 pltpu.VMEM((rows, width), BF16),
@@ -357,11 +352,10 @@
                 pltpu.VMEM((chunks, rows, CHUNK), BF16),
                 pltpu.VMEM((chunks, 2, edge, CHUNK), F32),
                 pltpu.VMEM((chunks, 2, edge, CHUNK), F32),
-                pltpu.VMEM((chunks, 2, edge, CHUNK // 2), F32),
+                pltpu.VMEM((chunks, 2, edge // 2, CHUNK), F32),
                 pltpu.VMEM((chunks, n, 8, CHUNK), F32),
                 pltpu.VMEM((chunks, n, 8, CHUNK), F32),
                 pltpu.SemaphoreType.DMA((2 + chunks,)),
-                pltpu.SemaphoreType.DMA((chunks,)),
                 pltpu.SemaphoreType.DMA((3, chunks, 2)),
                 pltpu.SemaphoreType.DMA((3, chunks, 2)),
                 pltpu.SemaphoreType.DMA((2, chunks, n - 1)),

time: 46.7 us -> 42.5 us (0.910)
  local copies, waits for them, and re-layouts: 4.73 us -> 0.97 us
    unnamed x7 -> x1, local copies, waits for them, and re-layouts: 4.73 us -> 0.97 us
where the time goes in v2:
time: 42.5 us; the launch traced here: 42.3 us
  Pallas kernels  40.7 us (96%)
  local copies, waits for them, and re-layouts  0.97 us (2%)
  between operations  0.66 us (2%)
    pallas_call x1, Pallas kernels, per_device(): pl.pallas_call(functools.partial(kernel, n), out_shape=pltpu.VMEM((rows,...  40.7 us
    unnamed x1, local copies, waits for them, and re-layouts  0.97 us

profile of v2, /device:TPU:0, one launch (start us, length us, event | category | flops | bytes accessed | tf_op | source)
XLA Modules:
  0.0 42.3 jit_solution(12224710342697974957)
XLA Ops:
  0.7 40.7 %shard_map.46 = f32[512,512]{1,0:T(8,128)S(1)} custom-call(f32[512,1024]{1,0:T(8,128)} %band_hbm.1, f32[512,128]{1,0:T(8,128)} %precond_hbm.1, s32[1]{0:T(128)S(6)} %copy.7.half_ref, f32[512,512]{1,0:T(8,128)} %rhs_hbm.1), custom_call_target="tpu_custom_call" | custom-call | tf_op jit(solution)/shard_map/pallas_call | solution.py:333
  41.3 1.0 %copy.6 = f32[512,512]{1,0:T(8,128)} copy(f32[512,512]{1,0:T(8,128)S(1)} %shard_map.46) | data formatting | bytes 2097152
